TPU v7x, 512 devices: a whole 4x4x16 slice. The times are simulated.
512 devices in a mesh: dp: 128 (over x, z, core), mp: 4 (over y).
Axes of the slice: x: 4, y: 4, z: 16, core: 2. Of those that a mesh axis runs over, the one named last changes fastest.
Arguments:
- frames: bfloat16 [32768, 2, 16, 256], P('dp', None, None, 'mp')
- cache: bfloat16 [32768, 2, 16, 256], P('dp', None, None, 'mp'), may hold values from -6 to 6
- group_offset: int32 [128], replicated, may hold values from 0 to 127, as said below
- cache_offset: int32 [128], replicated, may hold values from 0 to 127, as said below
- cache_group: int32 [128], replicated, may hold values from 0 to 127, each once
- group_rows: int32 [128, 128], P('dp'), may hold values from 1 to 2, 192 in all within a row
- cache_live: int32 [16384], P('dp'), may hold values 0 or 1
- temporal_weight: bfloat16 [3, 256, 512], P(None, None, 'mp')
- spatial_weight: bfloat16 [3, 512, 512], P(None, None, 'mp'), may hold values from -0.15625 to 0.15625
- norm_gain: bfloat16 [512], P('mp'), may hold values from 0.25 to 1.75
Outputs:
- latents: bfloat16 [32768, 2, 16, 512], P('dp', None, None, 'mp')
Inputs may be any that keep to these rules, and one draw needn't show every extreme that they name: group_offset[g] equals group_offset[g2] exactly when g - g2 is a multiple of 128. cache_offset[h] equals cache_offset[h2] exactly when h - h2 is a multiple of 128.
All inputs are finite; a program needn't handle non-finite values. No bound on the sum of `cache_live` on one device may be relied on, other than what follows from the above.
Results may differ from a plain program's by a relative error of at most 0.0026.
Values may be sent and summed in bfloat16 or wider, within the bound.
A program may use at most 128 MiB of HBM per device.

v0:
```python
import jax
import jax.numpy as jnp
from jax import lax
from jax.sharding import PartitionSpec as P


def temporal_conv(sequence, weight_part, span_steps):
    taps = weight_part.shape[0]
    windows = [
        sequence[:, taps - 1 - tap_index : taps - 1 - tap_index + span_steps]
        for tap_index in range(taps)
    ]
    joined = jnp.concatenate(windows, axis=3)
    flat_weight = weight_part.reshape((taps * weight_part.shape[1], weight_part.shape[2]))
    return jnp.einsum("rtwc,cd->rtwd", joined, flat_weight, preferred_element_type=jnp.float32)


def spatial_conv(activated, weight_part):
    width = activated.shape[2]
    padded = jnp.pad(activated, ((0, 0), (0, 0), (1, 1), (0, 0)))
    joined = jnp.concatenate(
        [padded[:, :, tap_index : tap_index + width] for tap_index in range(3)], axis=3
    )
    flat_weight = weight_part.reshape((3 * weight_part.shape[1], weight_part.shape[2]))
    return jnp.einsum("rtwc,cd->rtwd", joined, flat_weight, preferred_element_type=jnp.float32)


def to_slots(values, slot_index, owner_count, per_pair):
    buffer = (
        jnp.zeros((owner_count * per_pair,) + values.shape[1:], values.dtype)
        .at[slot_index]
        .set(values)
    )
    return buffer.reshape((owner_count, per_pair) + values.shape[1:])


def local(
    frames,
    cache,
    group_offset,
    cache_offset,
    cache_group,
    group_rows,
    cache_live,
    temporal_weight,
    spatial_weight,
    norm_gain,
):
    owner_count = lax.axis_size("dp")
    my_rank = lax.axis_index("dp")
    groups = group_offset.shape[0]
    pair_rows = frames.shape[0] // groups
    span_steps = frames.shape[1]
    per_pair = (groups + owner_count - 1) // owner_count
    group_index = jnp.arange(groups, dtype=jnp.int32)
    slot_level = group_index // owner_count
    grouped = frames.reshape((groups, pair_rows) + frames.shape[1:])
    counts = group_rows.reshape(groups)
    send_slot = (my_rank + group_offset) % owner_count * per_pair + slot_level
    got_rows, got_counts = (
        lax.all_to_all(
            to_slots(grouped, send_slot, owner_count, per_pair),
            "dp",
            split_axis=0,
            concat_axis=0,
            tiled=True,
        ),
        lax.all_to_all(
            to_slots(counts, send_slot, owner_count, per_pair),
            "dp",
            split_axis=0,
            concat_axis=0,
            tiled=True,
        ),
    )
    take_slot = (my_rank - group_offset) % owner_count * per_pair + slot_level
    own_rows = got_rows.reshape((owner_count * per_pair,) + grouped.shape[1:])[take_slot]
    own_counts = got_counts.reshape(owner_count * per_pair)[take_slot]
    cache_grouped = cache.reshape((groups, pair_rows) + cache.shape[1:])
    cache_send = (my_rank + cache_offset) % owner_count * per_pair + slot_level
    got_cache, got_flags = (
        lax.all_to_all(
            to_slots(cache_grouped, cache_send, owner_count, per_pair),
            "dp",
            split_axis=0,
            concat_axis=0,
            tiled=True,
        ),
        lax.all_to_all(
            to_slots(cache_live, cache_send, owner_count, per_pair),
            "dp",
            split_axis=0,
            concat_axis=0,
            tiled=True,
        ),
    )
    inverse = jnp.sum(
        group_index[:, None] * (cache_group[:, None] == group_index[None, :]).astype(jnp.int32),
        axis=0,
    )
    cache_slot = (my_rank - cache_offset[inverse]) % owner_count * per_pair + inverse // owner_count
    own_cache = got_cache.reshape((owner_count * per_pair,) + cache_grouped.shape[1:])[cache_slot]
    own_flags = got_flags.reshape(owner_count * per_pair)[cache_slot]
    own_cache = jnp.where(
        own_flags[:, None, None, None, None] > 0, own_cache, jnp.zeros_like(own_cache)
    )
    sequence = jnp.concatenate([own_cache, own_rows], axis=2)
    sequence = sequence.reshape((groups * pair_rows,) + sequence.shape[2:])
    live_rows = (jnp.arange(pair_rows, dtype=jnp.int32)[None, :] < own_counts[:, None]).reshape(
        groups * pair_rows
    )
    channels = spatial_weight.shape[1]
    weight_cut = temporal_weight
    conv_time = temporal_conv(
        lax.all_gather(sequence, "mp", axis=3, tiled=True), weight_cut, span_steps
    )
    square_sum = lax.psum(jnp.sum(conv_time * conv_time, axis=3), "mp")
    scaled = (
        conv_time
        * lax.rsqrt(square_sum / channels + 1e-06)[..., None]
        * norm_gain.astype(jnp.float32)
    )
    activated = jax.nn.silu(scaled).astype(jnp.bfloat16)
    weight_cut = spatial_weight
    conv_space = spatial_conv(lax.all_gather(activated, "mp", axis=3, tiled=True), weight_cut)
    latents = jnp.where(live_rows[:, None, None, None], conv_time + conv_space, 0.0).astype(
        jnp.bfloat16
    )
    return latents


def solution(mesh):
    in_specs = (
        P("dp", None, None, "mp"),
        P("dp", None, None, "mp"),
        P(),
        P(),
        P(),
        P("dp", None),
        P("dp"),
        P(None, None, "mp"),
        P(None, None, "mp"),
        P("mp"),
    )
    out_specs = P("dp", None, None, "mp")
    return jax.shard_map(local, mesh=mesh, in_specs=in_specs, out_specs=out_specs, check_vma=False)
```

profile of v0, /device:TPU:1, one launch (start us, length us, event | category | flops | bytes accessed | tf_op | source)
XLA Modules:
  0.0 459.1 jit_solution(11715463991772342249)
XLA Ops:
  9.1 20.4 %all-to-all-start.1 = ((s32[128,1,1]{2,1,0:T(1,128)}), s32[128,1,1]{2,1,0:T(1,128)S(1)}, u32[]{:S(2)}, u32[]{:S(2)}) async-start(s32[128,1,1]{2,1,0:T(1,128)} %copy.54), calls=%async_computation.1 | async-start | bytes 131072 | tf_op jit(solution)/shard_map/all_to_all | solution.py:89
  29.5 4.6 %copy.58 = bf16[256,2,16,64]{3,2,1,0:T(8,128)(2,1)} copy(bf16[256,2,16,64]{0,3,2,1:T(8,128)(2,1)} %param.10) | data formatting | bytes 2097152 | tf_op args[0]
  34.7 11.9 %scatter_fusion.1 = bf16[128,2,2,16,64]{4,3,2,1,0:T(8,128)(2,1)S(1)} fusion(bf16[128,2,2,16,64]{4,3,2,1,0:T(8,128)(2,1)S(1)} %broadcast.174.clone, s32[128]{0:T(128)S(1)} %get-tuple-element.11, bf16[128,2,2,16,64]{4,3,2,1,0:T(8,128)(2,1)} %bitcast.54), kind=kCustom, calls=%fused_computation.8 | custom fusion | bytes 3146240 | tf_op jit(solution)/shard_map/scatter | solution.py:32
  46.6 2.3 reshape.280
  49.5 16.2 %all-to-all-start.3 = ((bf16[128,2,2048]{2,1,0:T(2,128)(2,1)}), bf16[128,2,2048]{2,1,0:T(2,128)(2,1)S(1)}, u32[]{:S(2)}, u32[]{:S(2)}) async-start(bf16[128,2,2048]{2,1,0:T(2,128)(2,1)} %reshape.280), calls=%async_computation.3 | async-start | bytes 2097152 | tf_op jit(solution)/shard_map/all_to_all | solution.py:61
  65.7 4.6 %copy.55 = bf16[256,2,16,64]{3,2,1,0:T(8,128)(2,1)} copy(bf16[256,2,16,64]{0,3,2,1:T(8,128)(2,1)} %param.11) | data formatting | bytes 2097152 | tf_op args[1]
  70.9 11.9 %scatter_fusion = bf16[128,2,2,16,64]{4,3,2,1,0:T(8,128)(2,1)S(1)} fusion(bf16[128,2,2,16,64]{4,3,2,1,0:T(8,128)(2,1)S(1)} %broadcast.174.clone.1, s32[128]{0:T(128)S(1)} %get-tuple-element.14, bf16[128,2,2,16,64]{4,3,2,1,0:T(8,128)(2,1)} %bitcast.53), kind=kCustom, calls=%fused_computation.7 | custom fusion | bytes 3146240 | tf_op jit(solution)/shard_map/scatter | solution.py:32
  82.8 2.3 reshape.282
  85.2 34.9 %all-to-all-done.3 = bf16[128,2,2048]{2,1,0:T(2,128)(2,1)S(1)} async-done(((bf16[128,2,2048]{2,1,0:T(2,128)(2,1)}), bf16[128,2,2048]{2,1,0:T(2,128)(2,1)S(1)}, u32[]{:S(2)}, u32[]{:S(2)}) %all-to-all-start.3) | async-done | bytes 1048608 | tf_op jit(solution)/shard_map/all_to_all | solution.py:61
  120.1 8.9 %all-to-all-start.2 = ((bf16[128,2,2048]{2,1,0:T(2,128)(2,1)}), bf16[128,2,2048]{2,1,0:T(2,128)(2,1)}, u32[]{:S(2)}, u32[]{:S(2)}) async-start(bf16[128,2,2048]{2,1,0:T(2,128)(2,1)} %reshape.282), calls=%async_computation.2 | async-start | bytes 2097152 | tf_op jit(solution)/shard_map/all_to_all | solution.py:82
  130.5 3.2 reduce.1
  136.6 2.1 gather_fusion.4
  138.7 4.1 copy.60
  142.8 40.2 %all-to-all-done.2 = bf16[128,2,2048]{2,1,0:T(2,128)(2,1)} async-done(((bf16[128,2,2048]{2,1,0:T(2,128)(2,1)}), bf16[128,2,2048]{2,1,0:T(2,128)(2,1)}, u32[]{:S(2)}, u32[]{:S(2)}) %all-to-all-start.2) | async-done | bytes 1048608 | tf_op jit(solution)/shard_map/all_to_all | solution.py:82
  183.0 3.8 reshape.283
  186.8 2.1 gather_fusion.3
  189.0 4.1 copy.57
  194.7 84.3 %all-gather.3.cloned.1.call-done = bf16[256,4,16,256]{0,2,1,3:T(8,128)(2,1)} async-done(((bf16[256,4,16,64]{0,2,1,3:T(8,128)(2,1)}), bf16[256,4,16,256]{0,2,1,3:T(8,128)(2,1)}) %all-gather.3.cloned.1.call-update) | async-done | bytes 8388624 | tf_op jit(solution)/shard_map/all_gather | solution.py:115
  279.0 9.1 %fusion.30 = (bf16[256,2,16,256]{0,2,1,3:T(8,128)(2,1)}, bf16[256,2,16,256]{0,2,1,3:T(8,128)(2,1)}, bf16[256,2,16,256]{0,2,1,3:T(8,128)(2,1)}) fusion(bf16[256,4,16,256]{0,2,1,3:T(8,128)(2,1)} %all-gather.3.cloned.1.call-done), kind=kLoop, calls=%fused_computation.78 | loop fusion | bytes 25165824 | tf_op jit(solution)/shard_map/slice | solution.py:10
  288.1 7.5 %copy.73 = bf16[256,2,16,256]{3,0,2,1:T(8,128)(2,1)} copy(bf16[256,2,16,256]{0,2,1,3:T(8,128)(2,1)} %get-tuple-element.7) | data formatting | bytes 8388608
  295.6 7.5 %copy.74 = bf16[256,2,16,256]{3,0,2,1:T(8,128)(2,1)} copy(bf16[256,2,16,256]{0,2,1,3:T(8,128)(2,1)} %get-tuple-element.8) | data formatting | bytes 8388608
  303.1 7.6 %copy.75 = bf16[256,2,16,256]{3,0,2,1:T(8,128)(2,1)} copy(bf16[256,2,16,256]{0,2,1,3:T(8,128)(2,1)} %get-tuple-element.9) | data formatting | bytes 8388608
  310.7 8.5 %multiply_reduce_fusion = (f32[256,2,16]{0,2,1:T(8,128)S(1)}, f32[256,2,16,128]{0,3,2,1:T(8,128)}) fusion(bf16[768,128,1,1]{1,0,3,2:T(8,128)(2,1)S(1)} %bitcast.61, bf16[256,2,16,256]{3,0,2,1:T(8,128)(2,1)} %copy.75, bf16[256,2,16,256]{3,0,2,1:T(8,128)(2,1)} %copy.74, bf16[256,2,16,256]{3,0,2,1:T(8,128)(2,1)} %copy.73), kind=kOutput, calls=%fused_computation.25 | convolution fusion | flops 1650450432 | bytes 17006592 | tf_op jit(solution)/shard_map/rtwc,cd->rtwd/dot_general | solution.py:15
  319.2 12.0 %psum.7 = f32[256,2,16]{0,2,1:T(8,128)S(1)} all-reduce(f32[256,2,16]{0,2,1:T(8,128)S(1)} %get-tuple-element.12), channel_id=1, replica_groups=mesh['dp'=128,'mp'=4] {'mp'}, use_global_device_ids=true, to_apply=%region_6.7 | all-reduce | flops 8192 | bytes 65536 | tf_op jit(solution)/shard_map/psum | solution.py:117
  331.3 5.0 %multiply_convert_fusion = bf16[256,2,16,128]{0,3,2,1:T(8,128)(2,1)} fusion(f32[256,2,16,128]{0,3,2,1:T(8,128)} %get-tuple-element.13, f32[128]{0:T(128)S(1)} %convert_element_type.12, f32[256,2,16]{0,2,1:T(8,128)S(1)} %add_rsqrt_fusion), kind=kLoop, calls=%fused_computation.24 | loop fusion | flops 7340032 | bytes 6324736 | tf_op jit(solution)/shard_map/convert_element_type | solution.py:123
  337.5 35.5 %all_to_all.28 = s32[128,1,1]{2,1,0:T(1,128)S(1)} all-to-all(s32[128,1,1]{2,1,0:T(1,128)S(1)} %copy.53), channel_id=1, replica_groups=mesh['dp'=128,'mp'=4] {'dp'}, dimensions={0} | all-to-all | bytes 1024 | tf_op jit(solution)/shard_map/all_to_all | solution.py:68
  373.0 2.3 reduce
  376.9 54.2 %all-gather.5.cloned.1.call-done = bf16[256,2,16,512]{0,3,2,1:T(8,128)(2,1)} async-done(((bf16[256,2,16,128]{0,3,2,1:T(8,128)(2,1)}), bf16[256,2,16,512]{0,3,2,1:T(8,128)(2,1)}) %all-gather.5.cloned.1.call-update) | async-done | bytes 8388624 | tf_op jit(solution)/shard_map/all_gather | solution.py:125
  431.1 9.2 %pad_slice_fusion.1 = (bf16[256,2,16,512]{0,3,2,1:T(8,128)(2,1)S(1)}, bf16[256,2,16,512]{0,3,2,1:T(8,128)(2,1)}) fusion(bf16[256,2,16,512]{0,3,2,1:T(8,128)(2,1)} %all-gather.5.cloned.1.call-done), kind=kLoop, calls=%fused_computation.22 | loop fusion | bytes 25165824 | tf_op jit(solution)/shard_map/slice | solution.py:22
  440.3 1.8 copy-done.2
  442.1 7.1 %select_convert_fusion = bf16[256,2,16,128]{0,3,2,1:T(8,128)(2,1)S(1)} fusion(f32[256,2,16,128]{0,3,2,1:T(8,128)} %get-tuple-element.13, bf16[1536,128,1,1]{1,0,3,2:T(8,128)(2,1)S(1)} %bitcast.50, bf16[256,2,16,512]{0,3,2,1:T(8,128)(2,1)} %get-tuple-element.6, bf16[256,2,16,512]{0,3,2,1:T(8,128)(2,1)S(1)} %copy-done.2, ...), kind=kOutput, calls=%fused_computation.23 | convolution fusion | flops 3299868672 | bytes 31850752 | tf_op jit(solution)/shard_map/rtwc,cd->rtwd/dot_general | solution.py:25
  449.2 3.1 copy.67
  (46 shorter events, 12.9 us)
Async XLA Ops:
  6.5 433.7 %copy-start = (bf16[3,512,128]{2,1,0:T(8,128)(2,1)S(1)}, bf16[3,512,128]{2,1,0:T(8,128)(2,1)}, u32[]{:S(2)}) copy-start(bf16[3,512,128]{2,1,0:T(8,128)(2,1)} %param.18) | copy-start | bytes 1179652
  7.3 39.3 %copy-start.4 = (s32[128]{0:T(128)}, s32[128]{0:T(128)S(1)}, u32[]{:S(2)}) copy-start(s32[128]{0:T(128)S(1)} %get-tuple-element.11) | copy-start | bytes 1540
  9.1 39.8 %all-to-all-start.1 = ((s32[128,1,1]{2,1,0:T(1,128)}), s32[128,1,1]{2,1,0:T(1,128)S(1)}, u32[]{:S(2)}, u32[]{:S(2)}) async-start(s32[128,1,1]{2,1,0:T(1,128)} %copy.54), calls=%async_computation.1 | async-start | bytes 131072 | tf_op jit(solution)/shard_map/all_to_all | solution.py:89
  48.9 0.6 copy-start.3
  49.5 70.5 %all-to-all-start.3 = ((bf16[128,2,2048]{2,1,0:T(2,128)(2,1)}), bf16[128,2,2048]{2,1,0:T(2,128)(2,1)S(1)}, u32[]{:S(2)}, u32[]{:S(2)}) async-start(bf16[128,2,2048]{2,1,0:T(2,128)(2,1)} %reshape.280), calls=%async_computation.3 | async-start | bytes 2097152 | tf_op jit(solution)/shard_map/all_to_all | solution.py:61
  82.8 46.3 %copy-start.6 = (s32[128]{0:T(128)S(1)}, s32[128]{0:T(128)}, u32[]{:S(2)}) copy-start(s32[128]{0:T(128)} %param.14) | copy-start | bytes 1540
  82.8 46.4 %copy-start.1 = (s32[128]{0:T(128)S(1)}, s32[128]{0:T(128)}, u32[]{:S(2)}) copy-start(s32[128]{0:T(128)} %param.13) | copy-start | bytes 1540
  120.1 62.9 %all-to-all-start.2 = ((bf16[128,2,2048]{2,1,0:T(2,128)(2,1)}), bf16[128,2,2048]{2,1,0:T(2,128)(2,1)}, u32[]{:S(2)}, u32[]{:S(2)}) async-start(bf16[128,2,2048]{2,1,0:T(2,128)(2,1)} %reshape.282), calls=%async_computation.2 | async-start | bytes 2097152 | tf_op jit(solution)/shard_map/all_to_all | solution.py:82
  129.0 150.0 %all-gather.3.cloned.1.call-start = ((), (), s32[]{:S(2)}) async-start(), calls=%async_computation.4 | async-start | bytes 10485760 | tf_op jit(solution)/shard_map/all_gather | solution.py:115
  193.1 1.7 copy-start.7
  194.7 236.4 %all-gather.5.cloned.1.call-start = ((), (), s32[]{:S(2)}) async-start(), calls=%async_computation.5 | async-start | bytes 10485760 | tf_op jit(solution)/shard_map/all_gather | solution.py:125
  303.1 7.6 %copy-start.5 = (bf16[3,256,128]{2,1,0:T(8,128)(2,1)S(1)}, bf16[3,256,128]{2,1,0:T(8,128)(2,1)}, u32[]{:S(2)}) copy-start(bf16[3,256,128]{2,1,0:T(8,128)(2,1)} %param.17) | copy-start | bytes 589828
  431.1 11.0 %copy-start.2 = (bf16[256,2,16,512]{0,3,2,1:T(8,128)(2,1)S(1)}, bf16[256,2,16,512]{0,3,2,1:T(8,128)(2,1)}, u32[]{:S(2)}) copy-start(bf16[256,2,16,512]{0,3,2,1:T(8,128)(2,1)} %all-gather.5.cloned.1.call-done) | copy-start | bytes 25165828
Sparse Core Ops, SparseCore 0:
  194.8 84.1 all-gather.2
  336.4 94.5 all-gather.4
where the time goes:
time: 461 us; the launch traced here: 459 us
  waiting for transfers between devices  214 us (46%)
  local copies, waits for them, and re-layouts  110 us (24%)
  blocking collectives  47.5 us (10%)
  starting transfers between devices  45.6 us (10%)
  matrix products  15.7 us (3%)
  between operations  13.7 us (3%)
  other arithmetic  13.1 us (3%)
    all_gather x1, waiting for transfers between devices, local(): lax.all_gather(sequence, 'mp', axis=3, tiled=True)  84.3 us
    all_gather x1, waiting for transfers between devices, local(): lax.all_gather(activated, 'mp', axis=3, tiled=True)  54.2 us
    unnamed x25, local copies, waits for them, and re-layouts  44.1 us
    all_to_all x1, waiting for transfers between devices, local(): lax.all_to_all(to_slots(cache_grouped, cache_send, owner_count, per_pair)...  40.2 us
    all_to_all x1, blocking collectives, local(): lax.all_to_all(to_slots(counts, send_slot, owner_count, per_pair), 'dp',...  35.5 us
    all_to_all x1, waiting for transfers between devices, local(): lax.all_to_all(to_slots(grouped, send_slot, owner_count, per_pair), 'dp',...  34.9 us
    scatter x4, local copies, waits for them, and re-layouts, to_slots(): buffer = jnp.zeros((owner_count * per_pair,) + values.shape[1:], values.d...  26 us
    all_to_all x1, starting transfers between devices, local(): lax.all_to_all(to_slots(cache_live, cache_send, owner_count, per_pair), '...  20.4 us
  transfers between devices with their start and end apart: 5, of which 4 were waited for; matrix products, arithmetic and copies ran while one was open for 13% of the time, Pallas kernels for 0%

commit v1 on v0

v1 whole, which is shorter than its diff:
```python
import functools

import jax
import jax.numpy as jnp
from jax import lax
from jax.experimental import pallas as pl
from jax.experimental.pallas import tpu as pltpu
from jax.sharding import PartitionSpec as P

MESH = pl.DeviceIdType.MESH
EPS = 1e-6


def grid_of(owners):
    x_size = max(1, owners // 32)
    return x_size, owners // (2 * x_size)


def pair_number(source, owner, owners):
    x_size, z_size = grid_of(owners)
    half = z_size // 2
    dc = (owner % 2 - source % 2) % 2
    dz = (owner // 2 % z_size - source // 2 % z_size) % z_size
    dx = (owner // (2 * z_size) - source // (2 * z_size)) % x_size
    b = (dz >= half).astype(jnp.int32)
    h = jnp.where(dz >= half, z_size - 1 - dz, dz)
    c = (dx - h) % x_size
    return ((c * half + h) * 2 + dc) * 2 + b


def compute_slot(n, owners, ranks):
    half = grid_of(owners)[1] // 2
    b, dc, h, c = n % 2, n // 2 % 2, n // 4 % half, n // (4 * half)
    rank = (c + 2 * dc + h % 2) % ranks
    return rank * (owners // ranks) + c * half + h // 2 * 2 + b


def exchange_kernel(
    sizes, slot_of, keys, xc, xf, wt, ws, gn, out,
    wide, cache_out, frames_out, cache_in, cache_turn, carried, rows, wt_all, ws_all, gn_all, taps, result,
    w_send, w_recv, c_send, c_recv, f_send, f_recv, y_send, y_recv, o_send, o_recv,
):
    owners, ranks, pair, steps, width, cut, channels = sizes
    x_size, z_size = grid_of(owners)
    half = z_size // 2
    slots = owners // ranks
    part = channels // ranks
    c_in = cut * ranks
    lanes = steps * cut
    block = pair * width
    me, mine = lax.axis_index("dp"), lax.axis_index("mp")
    my_c, my_z, my_x = lax.rem(me, 2), lax.rem(lax.div(me, 2), z_size), lax.div(me, 2 * z_size)
    my_columns = pl.ds(pl.multiple_of(mine * part, part), part)

    def split(n):
        return lax.rem(n, 2), lax.rem(lax.div(n, 2), 2), lax.rem(lax.div(n, 4), half), lax.div(n, 4 * half)

    def owner_of(n):
        b, dc, h, c = split(n)
        z = lax.rem(my_z + h + b * (z_size - 1 - 2 * h), z_size)
        x = lax.rem(my_x + lax.rem(c + h, x_size), x_size)
        return (x * z_size + z) * 2 + lax.rem(my_c + dc, 2)

    weights = ((wt, wt_all), (ws, ws_all), (gn, gn_all))
    for index, (own, whole) in enumerate(weights):
        for turn in range(1, ranks):
            pltpu.make_async_remote_copy(
                own, whole.at[:, my_columns], w_send.at[index], w_recv.at[index],
                device_id=(me, lax.rem(mine + turn, ranks)), device_id_type=MESH,
            ).start()
        pltpu.make_async_copy(own, whole.at[:, my_columns], w_recv.at[index]).start()

    def pack(x, place, goes):
        for w in range(width):
            columns = jnp.concatenate(
                [x[(t * width + w) * cut : (t * width + w + 1) * cut, :] for t in range(steps)], axis=0
            )
            wide[pl.ds(w, owners * pair, stride=width), :] = lax.dot_general(
                place, columns, (((1,), (1,)), ((), ())), preferred_element_type=jnp.float32
            )

        per = min(16, owners)

        def narrow(i, _):
            piece = wide[pl.ds(pl.multiple_of(i * (per * block), per * block), per * block), :]
            goes[pl.ds(i * per, per)] = piece.astype(jnp.bfloat16).reshape(per, block, lanes)
            return 0

        lax.fori_loop(0, owners // per, narrow, 0)

    target = lax.broadcasted_iota(jnp.int32, (owners * pair, owners * pair), 0)
    pack(xc, jnp.where(target == keys[0:1, :], 1.0, 0.0).astype(jnp.bfloat16), cache_out)

    def send_cache(n, _):
        pltpu.make_async_remote_copy(
            cache_out.at[n], cache_in.at[n], c_send, c_recv, device_id=(owner_of(n), mine), device_id_type=MESH
        ).start()
        return 0

    lax.fori_loop(1, owners, send_cache, 0)

    live = jnp.where(keys[2:3, :] > 0, 1.0, jnp.nan)
    pack(xf, jnp.where(target == keys[1:2, :], live, 0.0).astype(jnp.bfloat16), frames_out)

    def frames_copy(n):
        b, dc, h, c = split(n)
        rank = lax.rem(c + 2 * dc + lax.rem(h, 2), ranks)
        place = c * half + lax.div(h, 2) * 2 + b
        return pltpu.make_async_remote_copy(
            frames_out.at[n], rows.at[mine, place], f_send, f_recv.at[c],
            device_id=(owner_of(n), rank), device_id_type=MESH,
        )

    @pl.when(mine == 0)
    def _():
        pltpu.make_async_copy(frames_out.at[0], rows.at[0, 0], f_recv.at[0]).start()

    @pl.when(mine != 0)
    def _():
        frames_copy(0).start()

    def send_frames(n, _):
        frames_copy(n).start()
        return 0

    lax.fori_loop(1, owners, send_frames, 0)

    for index, (own, whole) in enumerate(weights):
        pltpu.make_async_copy(whole, whole, w_recv.at[index]).wait()
    for m in range(ranks):
        tap = [wt_all[k * c_in + m * cut : k * c_in + (m + 1) * cut, :] for k in range(3)]
        nothing = jnp.zeros_like(tap[0])
        table = ((tap[0], tap[1]), (nothing, tap[0]), (tap[2], nothing), (tap[1], tap[2]))
        for q, (first, second) in enumerate(table):
            start = (q // 2 * ranks + m) * lanes + q % 2 * cut
            taps[start : start + cut, :channels] = first
            taps[start : start + cut, channels:] = second

    others = pl.ds(1, owners - 1)
    pltpu.make_async_copy(cache_in.at[others], cache_in.at[others], c_recv).wait()
    cache_in[0] = cache_out[0]

    def turn_cache(i, _):
        cache_turn[lax.div(i, slots), lax.rem(i, slots)] = cache_in[slot_of[i]]
        return 0

    lax.fori_loop(0, owners, turn_cache, 0)
    for turn in range(1, ranks):
        peer = lax.rem(mine + turn, ranks)
        pltpu.make_async_remote_copy(
            cache_turn.at[peer], carried.at[mine], y_send, y_recv, device_id=(me, peer), device_id_type=MESH
        ).start()
    pltpu.make_async_copy(cache_turn.at[mine], carried.at[mine], y_recv).start()
    pltpu.make_async_copy(carried, carried, y_recv).wait()

    gain = gn_all[0:1, :].astype(jnp.float32)
    tokens = half * block
    spot = lax.rem(lax.broadcasted_iota(jnp.int32, (steps * tokens, 1), 0), width)

    def encode(c, _):
        here = pl.ds(c * half, half)
        pltpu.make_async_copy(rows.at[:, here], rows.at[:, here], f_recv.at[c]).wait()
        pieces = [rows[m, here].reshape(tokens, lanes) for m in range(ranks)]
        dead = pieces[0][:, 0:1].astype(jnp.float32)
        dead = dead != dead
        pieces = pieces + [carried[m, here].reshape(tokens, lanes) for m in range(ranks)]
        both = jnp.dot(jnp.concatenate(pieces, axis=1), taps[...], preferred_element_type=jnp.float32)
        conv = jnp.concatenate([both[:, :channels], both[:, channels:]], axis=0)
        scale = lax.rsqrt(jnp.sum(conv * conv, axis=1, keepdims=True) / channels + EPS)
        scaled = conv * scale * gain
        active = scaled * (1.0 / (1.0 + jnp.exp(-scaled)))
        before = jnp.where(spot == 0, 0.0, pltpu.roll(active, 1, 0))
        after = jnp.where(spot == width - 1, 0.0, pltpu.roll(active, steps * tokens - 1, 0))
        joined = jnp.concatenate([v.astype(jnp.bfloat16) for v in (before, active, after)], axis=1)
        total = conv + jnp.dot(joined, ws_all[...], preferred_element_type=jnp.float32)
        total = jnp.where(jnp.concatenate([dead] * steps, axis=0), 0.0, total).astype(jnp.bfloat16)
        for m in range(ranks):
            for t in range(steps):
                piece = total[t * tokens : (t + 1) * tokens, m * part : (m + 1) * part]
                result[m, here, :, t] = piece.reshape(half, pair, width, part)
        for turn in range(1, ranks):
            peer = lax.rem(mine + turn, ranks)
            pltpu.make_async_remote_copy(
                result.at[peer, here], out.at[mine, here], o_send, o_recv, device_id=(me, peer), device_id_type=MESH
            ).start()
        pltpu.make_async_copy(result.at[mine, here], out.at[mine, here], o_recv).start()
        return 0

    lax.fori_loop(0, x_size, encode, 0)

    for index, (own, whole) in enumerate(weights):
        sent = whole.at[:, pl.ds(0, (ranks - 1) * part)]
        pltpu.make_async_copy(sent, sent, w_send.at[index]).wait()
    pltpu.make_async_copy(cache_out.at[others], cache_out.at[others], c_send).wait()

    @pl.when(mine == 0)
    def _():
        pltpu.make_async_copy(frames_out.at[others], frames_out.at[others], f_send).wait()

    @pl.when(mine != 0)
    def _():
        pltpu.make_async_copy(frames_out, frames_out, f_send).wait()

    sent = cache_turn.at[pl.ds(0, ranks - 1)]
    pltpu.make_async_copy(sent, sent, y_send).wait()
    sent = result.at[pl.ds(0, ranks - 1)]
    pltpu.make_async_copy(sent, sent, o_send).wait()
    pltpu.make_async_copy(out, out, o_recv).wait()


def order_kernel(per, slot_of, got, out):
    first = pl.program_id(0) * per

    def place(i, _):
        out[i] = got[slot_of[first + i]]
        return 0

    lax.fori_loop(0, per, place, 0)


def local(
    owners, ranks,
    frames, cache, group_offset, cache_offset, cache_group, group_rows, cache_live,
    temporal_weight, spatial_weight, norm_gain,
):
    me = lax.axis_index("dp")
    groups = group_offset.shape[0]
    pair = frames.shape[0] // groups
    steps, width, cut = frames.shape[1:]
    channels, part = spatial_weight.shape[1:]
    slots = owners // ranks
    group_index = jnp.arange(groups, dtype=jnp.int32)
    second = jnp.arange(pair, dtype=jnp.int32)[None, :]

    frames_to = pair_number(me, (me + group_offset) % owners, owners)
    cache_to = pair_number(me, (me + cache_offset) % owners, owners)
    keys = jnp.stack(
        [
            jnp.where(cache_live[:, None] > 0, cache_to[:, None] * pair + second, -1).reshape(-1),
            (frames_to[:, None] * pair + second).reshape(-1),
            (second < group_rows.reshape(groups)[:, None]).astype(jnp.int32).reshape(-1),
        ]
        + [jnp.zeros((groups * pair,), jnp.int32)] * 5
    )
    offset_here = jnp.sum(
        jnp.where(cache_group[:, None] == group_index[None, :], cache_offset[:, None], 0), axis=0
    )
    own_slot = compute_slot(pair_number((me - group_offset) % owners, me, owners), owners, ranks)
    from_cache = pair_number((me - offset_here) % owners, me, owners)
    cache_slot = jnp.sum(jnp.where(own_slot[:, None] == group_index[None, :], from_cache[:, None], 0), axis=0)

    rows_minor = lambda x: jnp.transpose(x, (1, 2, 3, 0)).reshape(steps * width * cut, groups * pair)
    block, lanes = pair * width, steps * cut
    vmem, smem, anywhere = (pl.BlockSpec(memory_space=s) for s in (pltpu.VMEM, pltpu.SMEM, pl.ANY))
    bf16 = jnp.bfloat16
    dma = pltpu.SemaphoreType.DMA
    got = pl.pallas_call(
        functools.partial(exchange_kernel, (owners, ranks, pair, steps, width, cut, channels)),
        out_shape=jax.ShapeDtypeStruct((ranks, slots, pair, steps, width, part), bf16),
        in_specs=[smem, vmem, vmem, vmem, anywhere, anywhere, anywhere],
        out_specs=anywhere,
        scratch_shapes=[
            pltpu.VMEM((owners * block, lanes), jnp.float32),
            pltpu.VMEM((owners, block, lanes), bf16),
            pltpu.VMEM((owners, block, lanes), bf16),
            pltpu.VMEM((owners, block, lanes), bf16),
            pltpu.VMEM((ranks, slots, block, lanes), bf16),
            pltpu.VMEM((ranks, slots, block, lanes), bf16),
            pltpu.VMEM((ranks, slots, block, lanes), bf16),
            pltpu.VMEM((3 * cut * ranks, channels), bf16),
            pltpu.VMEM((3 * channels, channels), bf16),
            pltpu.VMEM((16, channels), bf16),
            pltpu.VMEM((2 * ranks * lanes, steps * channels), bf16),
            pltpu.VMEM((ranks, slots, pair, steps, width, part), bf16),
            dma((3,)), dma((3,)), dma(()), dma(()), dma(()), dma((grid_of(owners)[0],)),
            dma(()), dma(()), dma(()), dma(()),
        ],
        compiler_params=pltpu.CompilerParams(has_side_effects=True, vmem_limit_bytes=48 << 20),
        name="exchange",
    )(
        cache_slot, keys, rows_minor(cache), rows_minor(frames),
        temporal_weight.reshape(-1, part), spatial_weight.reshape(-1, part),
        jnp.broadcast_to(norm_gain[None, :], (16, part)),
    )
    tokens = pair * steps * width
    per = min(32, groups)
    ordered = pl.pallas_call(
        functools.partial(order_kernel, per),
        out_shape=jax.ShapeDtypeStruct((groups, tokens, part), bf16),
        grid_spec=pltpu.PrefetchScalarGridSpec(
            num_scalar_prefetch=1,
            grid=(groups // per,),
            in_specs=[pl.BlockSpec((groups, tokens, part), lambda i, s: (0, 0, 0))],
            out_specs=pl.BlockSpec((per, tokens, part), lambda i, s: (i, 0, 0)),
        ),
        name="order",
    )(own_slot, got.reshape(groups, tokens, part))
    return ordered.reshape(groups * pair, steps, width, part)


def solution(mesh):
    in_specs = (
        P("dp", None, None, "mp"),
        P("dp", None, None, "mp"),
        P(),
        P(),
        P(),
        P("dp", None),
        P("dp"),
        P(None, None, "mp"),
        P(None, None, "mp"),
        P("mp"),
    )
    out_specs = P("dp", None, None, "mp")
    body = functools.partial(local, mesh.shape["dp"], mesh.shape["mp"])
    return jax.shard_map(body, mesh=mesh, in_specs=in_specs, out_specs=out_specs, check_vma=False)
```

time: 461 us -> 156 us (0.34)
  waiting for transfers between devices: 214 us -> 0 us
  Pallas kernels: 0 us -> 145 us
  local copies, waits for them, and re-layouts: 110 us -> 6.8 us
  blocking collectives: 47.5 us -> 0 us
  starting transfers between devices: 45.6 us -> 0 us
  matrix products: 15.7 us -> 0 us
  between operations: 13.7 us -> 0.09 us
  other arithmetic: 13.1 us -> 3.93 us
    pallas_call x0 -> x2, Pallas kernels: none -> 145 us  [the longest x1 140 us: local(): pl.pallas_call(functools.partial(exchange_kernel, (owners, ranks, pair, s...]
    all_gather x2 -> x0, waiting for transfers between devices: 138 us -> none  [the longest x1 84.3 us: local(): lax.all_gather(sequence, 'mp', axis=3, tiled=True)]
    all_to_all x3 -> x0, waiting for transfers between devices: 75.1 us -> none  [the longest x1 40.2 us: local(): lax.all_to_all(to_slots(cache_grouped, cache_send, owner_count, per_pair)...]
    all_to_all x3 -> x0, starting transfers between devices: 45.5 us -> none  [the longest x1 20.4 us: local(): lax.all_to_all(to_slots(cache_live, cache_send, owner_count, per_pair), '...]
    unnamed x25 -> x12, local copies, waits for them, and re-layouts: 44.1 us -> 5.7 us
    all_to_all x1 -> x0, blocking collectives: 35.5 us -> none  [local(): lax.all_to_all(to_slots(counts, send_slot, owner_count, per_pair), 'dp',...]
    scatter x4 -> x0, local copies, waits for them, and re-layouts: 26 us -> none  [to_slots(): buffer = jnp.zeros((owner_count * per_pair,) + values.shape[1:], values.d...]
    slice x2 -> x0, local copies, waits for them, and re-layouts: 18.3 us -> none  [the longest x1 9.17 us: spatial_conv(): padded[:, :, tap_index:tap_index + width]]
  transfers between devices with their start and end apart: 5 -> 0, of which waited for: 4 -> 0; matrix products, arithmetic and copies ran while one was open for 13% -> 0% of each run, Pallas kernels for 0% -> 0%
where the time goes in v1:
time: 156 us
  Pallas kernels  145 us (93%)
  local copies, waits for them, and re-layouts  6.8 us (4%)
  other arithmetic  3.93 us (3%)
    pallas_call x1, Pallas kernels, local(): pl.pallas_call(functools.partial(exchange_kernel, (owners, ranks, pair, s...  140 us
    unnamed x12, local copies, waits for them, and re-layouts  5.7 us
    pallas_call x1, Pallas kernels, local(): pl.pallas_call(functools.partial(order_kernel, per), out_shape=jax.ShapeD...  4.47 us

profile of v1, /device:TPU:1, one launch (start us, length us, event | category | flops | bytes accessed | tf_op | source)
XLA Modules:
  0.0 155.6 jit_solution(16600600626638670296)
XLA Ops:
  0.0 0.8 select_reduce_fusion.1
  0.8 0.7 broadcast_compare_fusion
  1.4 0.7 fusion.46
  2.2 0.7 fusion.62
  2.9 0.0 copy-start.5
  2.9 0.1 select_reduce_fusion.slot_of
  3.0 0.7 broadcast_in_dim.51.gn
  3.7 0.1 add_select_fusion
  3.8 0.1 select_n.327
  3.9 0.1 iota_add_fusion
  4.0 0.1 add.374
  4.2 0.7 fusion
  4.9 0.1 reshape.239
  5.1 0.0 copy-start.1
  5.1 1.2 copy-done.1
  6.3 0.0 copy-start.2
  6.3 1.2 copy-done.2
  7.5 0.0 copy-start.3
  7.5 1.0 copy-done.3
  8.5 0.0 copy-start.4
  8.5 0.9 copy-done.4
  9.5 140.3 %exchange.1 = bf16[4,32,2,2,16,128]{5,4,3,2,1,0:T(8,128)(2,1)S(1)} custom-call(s32[128]{0:T(128)S(1)} %select_reduce_fusion.slot_of, s32[8,256]{1,0:T(8,128)S(1)} %stack.7.keys, bf16[2048,256]{1,0:T(8,128)(2,1)S(1)} %bitcast.12, bf16[2048,256]{1,0:T(8,128)(2,1)S(1)} %bitcast.13, bf16[768,128]{1,0:T(8,128)(2,1)S(1)} %bitcast.15, ...), custom_call_target="tpu_custom_call" | custom-call | tf_op jit(solution)/shard_map/exchange/pallas_call | solution.py:257
  149.8 0.0 copy-done.5
  149.8 0.0 copy-start
  149.8 1.3 copy-done
  151.1 4.5 %order.1 = bf16[128,64,128]{2,1,0:T(8,128)(2,1)} custom-call(s32[128]{0:T(128)} %copy-done.5, bf16[128,64,128]{2,1,0:T(8,128)(2,1)} %bitcast.11), custom_call_target="tpu_custom_call" | custom-call | tf_op jit(solution)/shard_map/order/pallas_call | solution.py:287
  (3 shorter events, 0.0 us)
Async XLA Ops:
  2.9 146.9 %copy-start.5 = (s32[128]{0:T(128)}, s32[128]{0:T(128)S(1)}, u32[]{:S(2)}) copy-start(s32[128]{0:T(128)S(1)} %get-tuple-element.6.slot_of) | copy-start | bytes 1540
  5.1 1.2 copy-start.1
  6.3 1.2 copy-start.2
  7.5 1.0 copy-start.3
  8.5 0.9 copy-start.4
  149.8 1.3 copy-start

commit v2 on v1

v2 whole, which is shorter than its diff:
```python
import functools

import jax
import jax.numpy as jnp
from jax import lax
from jax.experimental import pallas as pl
from jax.experimental.pallas import tpu as pltpu
from jax.sharding import PartitionSpec as P

MESH = pl.DeviceIdType.MESH
EPS = 1e-6


def grid_of(owners):
    x_size = max(1, owners // 32)
    return x_size, owners // (2 * x_size)


def log2(size):
    return size.bit_length() - 1


def pair_number(source, owner, owners):
    x_size, z_size = grid_of(owners)
    half = z_size // 2
    dc = (owner - source) & 1
    dz = ((owner >> 1) - (source >> 1)) & (z_size - 1)
    dx = ((owner >> log2(2 * z_size)) - (source >> log2(2 * z_size))) & (x_size - 1)
    b = jnp.where(dz >= half, 1, 0)
    h = jnp.where(dz >= half, z_size - 1 - dz, dz)
    c = (dx - h) & (x_size - 1)
    return ((c * half + h) * 2 + dc) * 2 + b


def compute_slot(n, owners, ranks):
    half = grid_of(owners)[1] // 2
    b, dc, h, c = n & 1, (n >> 1) & 1, (n >> 2) & (half - 1), n >> log2(4 * half)
    rank = (c + 2 * dc + (h & 1)) & (ranks - 1)
    return rank * (owners // ranks) + c * half + (h >> 1) * 2 + b


def exchange_kernel(
    sizes, goes_to, cache_goes_to, continues, counts, lives, xc, xf, wt, ws, gn, out, order_out,
    table, picks, slot_row, slot_of, wide, xc_in, xf_in, gn_own, gn_row,
    cache_out, frames_out, cache_in, cache_turn, carried, rows, wt_all, ws_all, gn_all, taps, result,
    x_sem, t_sem, w_send, w_recv, c_send, c_recv, f_send, f_recv, y_send, y_recv, o_send, o_recv, ready,
):
    owners, ranks, pair, steps, width, cut, channels = sizes
    x_size, z_size = grid_of(owners)
    half = z_size // 2
    slots = owners // ranks
    stages = x_size * min(2, half // 2)
    part = channels // ranks
    c_in = cut * ranks
    lanes = steps * cut
    block = pair * width
    me, mine = lax.axis_index("dp"), lax.axis_index("mp")
    my_c, my_z, my_x = lax.rem(me, 2), lax.rem(lax.div(me, 2), z_size), lax.div(me, 2 * z_size)
    my_columns = pl.ds(pl.multiple_of(mine * part, part), part)
    bf16, f32 = jnp.bfloat16, jnp.float32

    loads = [
        pltpu.make_async_copy(own, here, x_sem.at[i])
        for i, (own, here) in enumerate(
            [(xc, xc_in), (xf, xf_in), (gn, gn_row)]
            + [(v, table.at[i]) for i, v in enumerate((goes_to, cache_goes_to, continues, counts, lives))]
        )
    ]
    for load in loads[3:] + loads[:3]:
        load.start()

    barrier = pltpu.get_barrier_semaphore()

    def greet(i, _):
        pl.semaphore_signal(barrier, inc=1, device_id=(lax.rem(me + i, owners), mine), device_id_type=MESH)
        return 0

    lax.fori_loop(1, owners, greet, 0)
    for turn in range(1, ranks):
        pl.semaphore_signal(
            barrier, inc=1, device_id=(me, lax.rem(mine + turn, ranks)), device_id_type=MESH
        )

    def split(n):
        return lax.rem(n, 2), lax.rem(lax.div(n, 2), 2), lax.rem(lax.div(n, 4), half), lax.div(n, 4 * half)

    def owner_of(n):
        b, dc, h, c = split(n)
        z = lax.rem(my_z + h + b * (z_size - 1 - 2 * h), z_size)
        x = lax.rem(my_x + lax.rem(c + h, x_size), x_size)
        return (x * z_size + z) * 2 + lax.rem(my_c + dc, 2)

    for load in loads[3:]:
        load.wait()
    group_to, cache_to, group_of, count, live = (table[i] for i in range(5))
    frames_n = pair_number(me, (me + group_to) & (owners - 1), owners)
    cache_n = pair_number(me, (me + cache_to) & (owners - 1), owners)
    sort = lax.broadcasted_iota(jnp.int32, (8, owners), 0)
    stack = jnp.where(sort == 0, frames_n, jnp.where(sort == 1, cache_n, jnp.where(sort == 2, count, live)))
    spread = lax.broadcasted_iota(jnp.int32, (owners, owners * pair), 1) >> log2(pair)
    spread = spread == lax.broadcasted_iota(jnp.int32, (owners, owners * pair), 0)
    one_hot = lambda mask: jnp.where(mask, 1.0, 0.0).astype(bf16)
    keys = jnp.dot(stack.astype(f32).astype(bf16), one_hot(spread), preferred_element_type=f32)
    second = (lax.broadcasted_iota(jnp.int32, (1, owners * pair), 1) & (pair - 1)).astype(f32)
    target = lax.broadcasted_iota(jnp.int32, (owners * pair, owners * pair), 0).astype(f32)

    def pack(x, place, goes):
        for w in range(width):
            columns = jnp.concatenate(
                [x[(t * width + w) * cut : (t * width + w + 1) * cut, :] for t in range(steps)], axis=0
            )
            wide[pl.ds(w, owners * pair, stride=width), :] = lax.dot_general(
                place, columns, (((1,), (1,)), ((), ())), preferred_element_type=f32
            )

        per = min(16, owners)

        def narrow(i, _):
            piece = wide[pl.ds(pl.multiple_of(i * (per * block), per * block), per * block), :]
            goes[pl.ds(i * per, per)] = piece.astype(bf16).reshape(per, block, lanes)
            return 0

        lax.fori_loop(0, owners // per, narrow, 0)

    loads[0].wait()
    pack(xc_in, jnp.where(target == keys[1:2, :] * pair + second, keys[3:4, :], 0.0).astype(bf16), cache_out)

    pl.semaphore_wait(barrier, owners - 1 + ranks - 1)
    for turn in range(1, ranks):
        pl.semaphore_signal(ready, inc=1, device_id=(me, lax.rem(mine + turn, ranks)), device_id_type=MESH)

    def send_cache(i, _):
        n = owners - 1 - i
        pltpu.make_async_remote_copy(
            cache_out.at[n], cache_in.at[n], c_send, c_recv, device_id=(owner_of(n), mine), device_id_type=MESH
        ).start()
        return 0

    lax.fori_loop(0, owners - 1, send_cache, 0)

    loads[1].wait()
    valid = jnp.where(second < keys[2:3, :], 1.0, jnp.nan)
    pack(xf_in, jnp.where(target == keys[0:1, :] * pair + second, valid, 0.0).astype(bf16), frames_out)

    def frames_copy(n):
        b, dc, h, c = split(n)
        rank = lax.rem(c + 2 * dc + lax.rem(h, 2), ranks)
        place = c * half + lax.div(h, 2) * 2 + b
        return pltpu.make_async_remote_copy(
            frames_out.at[n], rows.at[mine, place], f_send, f_recv.at[lax.div(n, owners // stages)],
            device_id=(owner_of(n), rank), device_id_type=MESH,
        )

    pl.semaphore_wait(ready, ranks - 1)

    def send_frames(i, _):
        frames_copy(owners - 1 - i).start()
        return 0

    lax.fori_loop(0, owners - 1, send_frames, 0)

    @pl.when(mine == 0)
    def _():
        pltpu.make_async_copy(frames_out.at[0], rows.at[0, 0], f_recv.at[0]).start()

    @pl.when(mine != 0)
    def _():
        frames_copy(0).start()

    loads[2].wait()
    gn_own[...] = jnp.broadcast_to(gn_row[...].astype(f32), gn_own.shape).astype(bf16)
    weights = ((wt, wt_all), (ws, ws_all), (gn_own, gn_all))
    for index, (own, whole) in enumerate(weights):
        for turn in range(1, ranks):
            pltpu.make_async_remote_copy(
                own, whole.at[:, my_columns], w_send.at[index], w_recv.at[index],
                device_id=(me, lax.rem(mine + turn, ranks)), device_id_type=MESH,
            ).start()
        pltpu.make_async_copy(own, whole.at[:, my_columns], w_recv.at[index]).start()

    own_n = pair_number((me - group_to) & (owners - 1), me, owners)
    own_slot = compute_slot(own_n, owners, ranks)
    slot_row[...] = own_slot
    slot_store = pltpu.make_async_copy(slot_row, order_out, t_sem.at[1])
    slot_store.start()
    line = lax.broadcasted_iota(jnp.int32, (owners, owners), 0)

    def choose(values, mask):
        values = jnp.broadcast_to(values.astype(f32), (8, owners)).astype(bf16)
        got = lax.dot_general(values, one_hot(mask), (((1,), (1,)), ((), ())), preferred_element_type=f32)
        return got[0:1, :].astype(jnp.int32)

    cache_here = choose(cache_to, line == group_of)
    cache_from = pair_number((me - cache_here) & (owners - 1), me, owners)
    picks[...] = choose(cache_from, line == own_slot)
    pick_load = pltpu.make_async_copy(picks, slot_of, t_sem.at[0])
    pick_load.start()

    for index, (own, whole) in enumerate(weights):
        pltpu.make_async_copy(whole, whole, w_recv.at[index]).wait()
    for m in range(ranks):
        tap = [wt_all[k * c_in + m * cut : k * c_in + (m + 1) * cut, :] for k in range(3)]
        nothing = jnp.zeros_like(tap[0])
        table = ((tap[0], tap[1]), (nothing, tap[0]), (tap[2], nothing), (tap[1], tap[2]))
        for q, (first, second) in enumerate(table):
            start = (q // 2 * ranks + m) * lanes + q % 2 * cut
            taps[start : start + cut, :channels] = first
            taps[start : start + cut, channels:] = second

    others = pl.ds(1, owners - 1)
    pltpu.make_async_copy(cache_in.at[others], cache_in.at[others], c_recv).wait()
    cache_in[0] = cache_out[0]

    pick_load.wait()

    def turn_cache(i, _):
        cache_turn[lax.div(i, slots), lax.rem(i, slots)] = cache_in[jnp.minimum(jnp.maximum(slot_of[0, i], 0), owners - 1)]
        return 0

    lax.fori_loop(0, owners, turn_cache, 0)
    for turn in range(1, ranks):
        peer = lax.rem(mine + turn, ranks)
        pltpu.make_async_remote_copy(
            cache_turn.at[peer], carried.at[mine], y_send, y_recv, device_id=(me, peer), device_id_type=MESH
        ).start()
    pltpu.make_async_copy(cache_turn.at[mine], carried.at[mine], y_recv).start()
    pltpu.make_async_copy(carried, carried, y_recv).wait()

    gain = gn_all[0:1, :].astype(jnp.float32)
    size = slots // stages
    tokens = size * block
    spot = lax.rem(lax.broadcasted_iota(jnp.int32, (steps * tokens, 1), 0), width)

    def encode(i, _):
        stage = stages - 1 - i
        here = pl.ds(stage * size, size)
        pltpu.make_async_copy(rows.at[:, here], rows.at[:, here], f_recv.at[stage]).wait()
        pieces = [rows[m, here].reshape(tokens, lanes) for m in range(ranks)]
        dead = pieces[0][:, 0:1].astype(jnp.float32)
        dead = dead != dead
        pieces = pieces + [carried[m, here].reshape(tokens, lanes) for m in range(ranks)]
        both = jnp.dot(jnp.concatenate(pieces, axis=1), taps[...], preferred_element_type=jnp.float32)
        conv = jnp.concatenate([both[:, :channels], both[:, channels:]], axis=0)
        scale = lax.rsqrt(jnp.sum(conv * conv, axis=1, keepdims=True) / channels + EPS)
        scaled = conv * scale * gain
        active = scaled * (1.0 / (1.0 + jnp.exp(-scaled)))
        before = jnp.where(spot == 0, 0.0, pltpu.roll(active, 1, 0))
        after = jnp.where(spot == width - 1, 0.0, pltpu.roll(active, steps * tokens - 1, 0))
        joined = jnp.concatenate([v.astype(jnp.bfloat16) for v in (before, active, after)], axis=1)
        total = conv + jnp.dot(joined, ws_all[...], preferred_element_type=jnp.float32)
        total = jnp.where(jnp.concatenate([dead] * steps, axis=0), 0.0, total).astype(jnp.bfloat16)
        for m in range(ranks):
            for t in range(steps):
                piece = total[t * tokens : (t + 1) * tokens, m * part : (m + 1) * part]
                result[m, here, :, t] = piece.reshape(size, pair, width, part)
        for turn in range(1, ranks):
            peer = lax.rem(mine + turn, ranks)
            pltpu.make_async_remote_copy(
                result.at[peer, here], out.at[mine, here], o_send, o_recv, device_id=(me, peer), device_id_type=MESH
            ).start()
        pltpu.make_async_copy(result.at[mine, here], out.at[mine, here], o_recv).start()
        return 0

    lax.fori_loop(0, stages, encode, 0)

    for index, (own, whole) in enumerate(weights):
        sent = whole.at[:, pl.ds(0, (ranks - 1) * part)]
        pltpu.make_async_copy(sent, sent, w_send.at[index]).wait()
    pltpu.make_async_copy(cache_out.at[others], cache_out.at[others], c_send).wait()

    @pl.when(mine == 0)
    def _():
        pltpu.make_async_copy(frames_out.at[others], frames_out.at[others], f_send).wait()

    @pl.when(mine != 0)
    def _():
        pltpu.make_async_copy(frames_out, frames_out, f_send).wait()

    sent = cache_turn.at[pl.ds(0, ranks - 1)]
    pltpu.make_async_copy(sent, sent, y_send).wait()
    sent = result.at[pl.ds(0, ranks - 1)]
    pltpu.make_async_copy(sent, sent, o_send).wait()
    slot_store.wait()
    pltpu.make_async_copy(out, out, o_recv).wait()


def order_kernel(slot_of, got, out, sem):
    def place(i, _):
        pltpu.make_async_copy(got.at[slot_of[0, i]], out.at[i], sem).start()
        return 0

    lax.fori_loop(0, out.shape[0], place, 0)
    pltpu.make_async_copy(got, out, sem).wait()


def local(
    owners, ranks,
    frames, cache, group_offset, cache_offset, cache_group, group_rows, cache_live,
    temporal_weight, spatial_weight, norm_gain,
):
    groups = group_offset.shape[0]
    pair = frames.shape[0] // groups
    steps, width, cut = frames.shape[1:]
    channels, part = spatial_weight.shape[1:]
    slots = owners // ranks
    stages = grid_of(owners)[0] * min(2, grid_of(owners)[1] // 4)
    rows_minor = lambda x: jnp.transpose(x, (1, 2, 3, 0)).reshape(steps * width * cut, groups * pair)
    line = lambda x: x.reshape(1, groups)
    block, lanes, tokens = pair * width, steps * cut, pair * steps * width
    smem, hbm = (pl.BlockSpec(memory_space=s) for s in (pltpu.SMEM, pltpu.HBM))
    bf16 = jnp.bfloat16
    dma = pltpu.SemaphoreType.DMA
    got, own_slot = pl.pallas_call(
        functools.partial(exchange_kernel, (owners, ranks, pair, steps, width, cut, channels)),
        out_shape=(
            jax.ShapeDtypeStruct((ranks, slots, pair, steps, width, part), bf16),
            jax.ShapeDtypeStruct((1, groups), jnp.int32),
        ),
        in_specs=[hbm] * 10,
        out_specs=(hbm, hbm),
        scratch_shapes=[
            pltpu.VMEM((5, 1, groups), jnp.int32),
            pltpu.VMEM((1, groups), jnp.int32),
            pltpu.VMEM((1, groups), jnp.int32),
            pltpu.SMEM((1, groups), jnp.int32),
            pltpu.VMEM((owners * block, lanes), jnp.float32),
            pltpu.VMEM((steps * width * cut, groups * pair), bf16),
            pltpu.VMEM((steps * width * cut, groups * pair), bf16),
            pltpu.VMEM((16, part), bf16),
            pltpu.VMEM((1, part), bf16),
            pltpu.VMEM((owners, block, lanes), bf16),
            pltpu.VMEM((owners, block, lanes), bf16),
            pltpu.VMEM((owners, block, lanes), bf16),
            pltpu.VMEM((ranks, slots, block, lanes), bf16),
            pltpu.VMEM((ranks, slots, block, lanes), bf16),
            pltpu.VMEM((ranks, slots, block, lanes), bf16),
            pltpu.VMEM((3 * cut * ranks, channels), bf16),
            pltpu.VMEM((3 * channels, channels), bf16),
            pltpu.VMEM((16, channels), bf16),
            pltpu.VMEM((2 * ranks * lanes, steps * channels), bf16),
            pltpu.VMEM((ranks, slots, pair, steps, width, part), bf16),
            dma((8,)), dma((2,)), dma((3,)), dma((3,)), dma(()), dma(()), dma(()), dma((stages,)),
            dma(()), dma(()), dma(()), dma(()), pltpu.SemaphoreType.REGULAR,
        ],
        compiler_params=pltpu.CompilerParams(
            collective_id=0, has_side_effects=True, vmem_limit_bytes=60 << 20
        ),
        name="exchange",
    )(
        line(group_offset), line(cache_offset), line(cache_group), line(group_rows), line(cache_live),
        rows_minor(cache), rows_minor(frames),
        temporal_weight.reshape(-1, part), spatial_weight.reshape(-1, part), norm_gain.reshape(1, part),
    )
    ordered = pl.pallas_call(
        order_kernel,
        out_shape=jax.ShapeDtypeStruct((groups, tokens, part), bf16),
        in_specs=[smem, hbm],
        out_specs=hbm,
        scratch_shapes=[dma(())],
        compiler_params=pltpu.CompilerParams(vmem_limit_bytes=60 << 20),
        name="order",
    )(own_slot, got.reshape(groups, tokens, part))
    return ordered.reshape(groups * pair, steps, width, part)


def solution(mesh):
    in_specs = (
        P("dp", None, None, "mp"),
        P("dp", None, None, "mp"),
        P(),
        P(),
        P(),
        P("dp", None),
        P("dp"),
        P(None, None, "mp"),
        P(None, None, "mp"),
        P("mp"),
    )
    out_specs = P("dp", None, None, "mp")
    body = functools.partial(local, mesh.shape["dp"], mesh.shape["mp"])
    return jax.shard_map(body, mesh=mesh, in_specs=in_specs, out_specs=out_specs, check_vma=False)
```

time: 156 us -> 186 us (1.19)
  Pallas kernels: 145 us -> 186 us
  local copies, waits for them, and re-layouts: 6.8 us -> 0 us
  other arithmetic: 3.93 us -> 0 us
    pallas_call x1, Pallas kernels: 4.47 us -> 65.3 us  [local(): pl.pallas_call(order_kernel, out_shape=jax.ShapeDtypeStruct((groups, toke...]
    pallas_call x1, Pallas kernels: 140 us -> 121 us  [local(): pl.pallas_call(functools.partial(exchange_kernel, (owners, ranks, pair, s...]
    unnamed x12 -> x0, local copies, waits for them, and re-layouts: 5.7 us -> none
where the time goes in v2:
time: 186 us
  Pallas kernels  186 us (100%)
    pallas_call x1, Pallas kernels, local(): pl.pallas_call(functools.partial(exchange_kernel, (owners, ranks, pair, s...  121 us
    pallas_call x1, Pallas kernels, local(): pl.pallas_call(order_kernel, out_shape=jax.ShapeDtypeStruct((groups, toke...  65.3 us

profile of v2, /device:TPU:1, one launch (start us, length us, event | category | flops | bytes accessed | tf_op | source)
XLA Modules:
  0.0 186.1 jit_solution(3514363693736844089)
XLA Ops:
  0.0 120.8 %exchange.1 = (bf16[4,32,2,2,16,128]{5,4,3,2,1,0:T(8,128)(2,1)}, s32[1,128]{1,0:T(1,128)}) custom-call(s32[1,128]{1,0:T(1,128)} %bitcast.20, s32[1,128]{1,0:T(1,128)} %bitcast.21, s32[1,128]{1,0:T(1,128)} %bitcast.22, s32[1,128]{1,0:T(1,128)} %counts.1, s32[1,128]{1,0:T(1,128)} %bitcast.23, bf16[2048,256]{1,0:T(8,128)(2,1)} %bitcast.16, ...), custom_call_target="tpu_custom_call" | custom-call | tf_op jit(solution)/shard_map/exchange/pallas_call | solution.py:313
  120.8 65.3 %order.1 = bf16[128,64,128]{2,1,0:T(8,128)(2,1)} custom-call(s32[1,128]{1,0:T(1,128)} %get-tuple-element.7.slot_of, bf16[128,64,128]{2,1,0:T(8,128)(2,1)} %bitcast.15), custom_call_target="tpu_custom_call" | custom-call | tf_op jit(solution)/shard_map/order/pallas_call | solution.py:354

commit v3 on v2

--- a/solution.py
+++ b/solution.py
@@ -284,13 +284,25 @@
     pltpu.make_async_copy(out, out, o_recv).wait()
 
 
-def order_kernel(slot_of, got, out, sem):
+def order_kernel(slot_of, got, out, held, load_sem, store_sem):
+    quarter = held.shape[0] // 4
+    loads = [
+        pltpu.make_async_copy(
+            got.at[pl.ds(i * quarter, quarter)], held.at[pl.ds(i * quarter, quarter)], load_sem.at[i]
+        )
+        for i in range(4)
+    ]
+    for load in loads:
+        load.start()
+    for load in loads:
+        load.wait()
+
     def place(i, _):
-        pltpu.make_async_copy(got.at[slot_of[0, i]], out.at[i], sem).start()
+        pltpu.make_async_copy(held.at[slot_of[0, i]], out.at[i], store_sem).start()
         return 0
 
     lax.fori_loop(0, out.shape[0], place, 0)
-    pltpu.make_async_copy(got, out, sem).wait()
+    pltpu.make_async_copy(held, out, store_sem).wait()
 
 
 def local(
@@ -356,7 +368,7 @@
         out_shape=jax.ShapeDtypeStruct((groups, tokens, part), bf16),
         in_specs=[smem, hbm],
         out_specs=hbm,
-        scratch_shapes=[dma(())],
+        scratch_shapes=[pltpu.VMEM((groups, tokens, part), bf16), dma((4,)), dma(())],
         compiler_params=pltpu.CompilerParams(vmem_limit_bytes=60 << 20),
         name="order",
     )(own_slot, got.reshape(groups, tokens, part))

time: 186 us -> 124 us (0.67)
  Pallas kernels: 186 us -> 124 us
    pallas_call x1, Pallas kernels: 65.3 us -> 3.49 us  [local(): pl.pallas_call(order_kernel, out_shape=jax.ShapeDtypeStruct((groups, toke...]
where the time goes in v3:
time: 124 us
  Pallas kernels  124 us (100%)
    pallas_call x1, Pallas kernels, local(): pl.pallas_call(functools.partial(exchange_kernel, (owners, ranks, pair, s...  121 us
    pallas_call x1, Pallas kernels, local(): pl.pallas_call(order_kernel, out_shape=jax.ShapeDtypeStruct((groups, toke...  3.49 us

profile of v3, /device:TPU:1, one launch (start us, length us, event | category | flops | bytes accessed | tf_op | source)
XLA Modules:
  0.0 124.3 jit_solution(4477238657563253786)
XLA Ops:
  0.0 120.8 %exchange.1 = (bf16[4,32,2,2,16,128]{5,4,3,2,1,0:T(8,128)(2,1)}, s32[1,128]{1,0:T(1,128)}) custom-call(s32[1,128]{1,0:T(1,128)} %bitcast.20, s32[1,128]{1,0:T(1,128)} %bitcast.21, s32[1,128]{1,0:T(1,128)} %bitcast.22, s32[1,128]{1,0:T(1,128)} %counts.1, s32[1,128]{1,0:T(1,128)} %bitcast.23, bf16[2048,256]{1,0:T(8,128)(2,1)} %bitcast.16, ...), custom_call_target="tpu_custom_call" | custom-call | tf_op jit(solution)/shard_map/exchange/pallas_call | solution.py:325
  120.8 3.5 %order.1 = bf16[128,64,128]{2,1,0:T(8,128)(2,1)} custom-call(s32[1,128]{1,0:T(1,128)} %get-tuple-element.7.slot_of, bf16[128,64,128]{2,1,0:T(8,128)(2,1)} %bitcast.15), custom_call_target="tpu_custom_call" | custom-call | tf_op jit(solution)/shard_map/order/pallas_call | solution.py:366

commit v4 on v2

--- a/solution.py
+++ b/solution.py
@@ -35,7 +35,7 @@
 def compute_slot(n, owners, ranks):
     half = grid_of(owners)[1] // 2
     b, dc, h, c = n & 1, (n >> 1) & 1, (n >> 2) & (half - 1), n >> log2(4 * half)
-    rank = (c + 2 * dc + (h & 1)) & (ranks - 1)
+    rank = (c + 2 * dc + ((h + (h >> 1)) & 1)) & (ranks - 1)
     return rank * (owners // ranks) + c * half + (h >> 1) * 2 + b
 
 
@@ -49,7 +49,7 @@
     x_size, z_size = grid_of(owners)
     half = z_size // 2
     slots = owners // ranks
-    stages = x_size * min(2, half // 2)
+    stages = x_size * half // 2
     part = channels // ranks
     c_in = cut * ranks
     lanes = steps * cut
@@ -58,6 +58,17 @@
     my_c, my_z, my_x = lax.rem(me, 2), lax.rem(lax.div(me, 2), z_size), lax.div(me, 2 * z_size)
     my_columns = pl.ds(pl.multiple_of(mine * part, part), part)
     bf16, f32 = jnp.bfloat16, jnp.float32
+
+    def split(n):
+        if isinstance(n, int):
+            return n % 2, n // 2 % 2, n // 4 % half, n // (4 * half)
+        return lax.rem(n, 2), lax.rem(lax.div(n, 2), 2), lax.rem(lax.div(n, 4), half), lax.div(n, 4 * half)
+
+    def owner_of(n):
+        b, dc, h, c = split(n)
+        z = lax.rem(my_z + h + b * (z_size - 1 - 2 * h), z_size)
+        x = lax.rem(my_x + c + h, x_size)
+        return (x * z_size + z) * 2 + lax.rem(my_c + dc, 2)
 
     loads = [
         pltpu.make_async_copy(own, here, x_sem.at[i])
@@ -71,24 +82,21 @@
 
     barrier = pltpu.get_barrier_semaphore()
 
-    def greet(i, _):
-        pl.semaphore_signal(barrier, inc=1, device_id=(lax.rem(me + i, owners), mine), device_id_type=MESH)
-        return 0
-
-    lax.fori_loop(1, owners, greet, 0)
+    def greet():
+        for i in range(owners - 1):
+            turn, low = i // (4 * x_size), i % 4
+            n = i // 4 % x_size * (4 * half) + (half - 1 - turn) * 4 + 3 - low
+            if turn == half - 1:
+                c, low = divmod(i - turn * 4 * x_size, 4) if i < owners - 4 else (x_size - 1, i - owners + 4)
+                c = x_size - 1 - c
+                n = c * 4 * half + 3 - low
+            pl.semaphore_signal(barrier, inc=1, device_id=(owner_of(n), mine), device_id_type=MESH)
+
+    greet()
     for turn in range(1, ranks):
         pl.semaphore_signal(
             barrier, inc=1, device_id=(me, lax.rem(mine + turn, ranks)), device_id_type=MESH
         )
-
-    def split(n):
-        return lax.rem(n, 2), lax.rem(lax.div(n, 2), 2), lax.rem(lax.div(n, 4), half), lax.div(n, 4 * half)
-
-    def owner_of(n):
-        b, dc, h, c = split(n)
-        z = lax.rem(my_z + h + b * (z_size - 1 - 2 * h), z_size)
-        x = lax.rem(my_x + lax.rem(c + h, x_size), x_size)
-        return (x * z_size + z) * 2 + lax.rem(my_c + dc, 2)
 
     for load in loads[3:]:
         load.wait()
@@ -144,7 +152,7 @@
 
     def frames_copy(n):
         b, dc, h, c = split(n)
-        rank = lax.rem(c + 2 * dc + lax.rem(h, 2), ranks)
+        rank = lax.rem(c + 2 * dc + lax.rem(h + lax.div(h, 2), 2), ranks)
         place = c * half + lax.div(h, 2) * 2 + b
         return pltpu.make_async_remote_copy(
             frames_out.at[n], rows.at[mine, place], f_send, f_recv.at[lax.div(n, owners // stages)],
@@ -284,13 +292,24 @@
     pltpu.make_async_copy(out, out, o_recv).wait()
 
 
-def order_kernel(slot_of, got, out, sem):
-    def place(i, _):
-        pltpu.make_async_copy(got.at[slot_of[0, i]], out.at[i], sem).start()
+def order_kernel(slot_of, got, out, held, ordered, load_sem, store_sem):
+    load = pltpu.make_async_copy(got, held, load_sem)
+    load.start()
+    load.wait()
+    count = store_sem.shape[0]
+    size = held.shape[0] // count
+
+    def place(q, _):
+        for i in range(size):
+            ordered[q * size + i] = held[slot_of[0, q * size + i]]
+        here = pl.ds(q * size, size)
+        pltpu.make_async_copy(ordered.at[here], out.at[here], store_sem.at[q]).start()
         return 0
 
-    lax.fori_loop(0, out.shape[0], place, 0)
-    pltpu.make_async_copy(got, out, sem).wait()
+    lax.fori_loop(0, count, place, 0)
+    for q in range(count):
+        here = pl.ds(q * size, size)
+        pltpu.make_async_copy(ordered.at[here], out.at[here], store_sem.at[q]).wait()
 
 
 def local(
@@ -303,7 +322,7 @@
     steps, width, cut = frames.shape[1:]
     channels, part = spatial_weight.shape[1:]
     slots = owners // ranks
-    stages = grid_of(owners)[0] * min(2, grid_of(owners)[1] // 4)
+    stages = grid_of(owners)[0] * grid_of(owners)[1] // 4
     rows_minor = lambda x: jnp.transpose(x, (1, 2, 3, 0)).reshape(steps * width * cut, groups * pair)
     line = lambda x: x.reshape(1, groups)
     block, lanes, tokens = pair * width, steps * cut, pair * steps * width
@@ -356,7 +375,7 @@
         out_shape=jax.ShapeDtypeStruct((groups, tokens, part), bf16),
         in_specs=[smem, hbm],
         out_specs=hbm,
-        scratch_shapes=[dma(())],
+        scratch_shapes=[pltpu.VMEM((groups, tokens, part), bf16)] * 2 + [dma(()), dma((4,))],
         compiler_params=pltpu.CompilerParams(vmem_limit_bytes=60 << 20),
         name="order",
     )(own_slot, got.reshape(groups, tokens, part))

time: 186 us -> 121 us (0.65)
  Pallas kernels: 186 us -> 121 us
    pallas_call x1, Pallas kernels: 65.3 us -> 3.64 us  [local(): pl.pallas_call(order_kernel, out_shape=jax.ShapeDtypeStruct((groups, toke...]
    pallas_call x1, Pallas kernels: 121 us -> 118 us  [local(): pl.pallas_call(functools.partial(exchange_kernel, (owners, ranks, pair, s...]
where the time goes in v4:
time: 121 us
  Pallas kernels  121 us (100%)
    pallas_call x1, Pallas kernels, local(): pl.pallas_call(functools.partial(exchange_kernel, (owners, ranks, pair, s...  118 us
    pallas_call x1, Pallas kernels, local(): pl.pallas_call(order_kernel, out_shape=jax.ShapeDtypeStruct((groups, toke...  3.64 us

profile of v4, /device:TPU:1, one launch (start us, length us, event | category | flops | bytes accessed | tf_op | source)
XLA Modules:
  0.0 121.3 jit_solution(7737312947918338592)
XLA Ops:
  0.0 117.6 %exchange.1 = (bf16[4,32,2,2,16,128]{5,4,3,2,1,0:T(8,128)(2,1)}, s32[1,128]{1,0:T(1,128)}) custom-call(s32[1,128]{1,0:T(1,128)} %bitcast.20, s32[1,128]{1,0:T(1,128)} %bitcast.21, s32[1,128]{1,0:T(1,128)} %bitcast.22, s32[1,128]{1,0:T(1,128)} %counts.1, s32[1,128]{1,0:T(1,128)} %bitcast.23, bf16[2048,256]{1,0:T(8,128)(2,1)} %bitcast.16, ...), custom_call_target="tpu_custom_call" | custom-call | tf_op jit(solution)/shard_map/exchange/pallas_call | solution.py:332
  117.6 3.6 %order.1 = bf16[128,64,128]{2,1,0:T(8,128)(2,1)} custom-call(s32[1,128]{1,0:T(1,128)} %get-tuple-element.7.slot_of, bf16[128,64,128]{2,1,0:T(8,128)(2,1)} %bitcast.15), custom_call_target="tpu_custom_call" | custom-call | tf_op jit(solution)/shard_map/order/pallas_call | solution.py:373
